TPU v7x, 512 devices: a whole 4x8x8 slice. The times are simulated.
512 devices in a mesh: dp: 4 (over z_lo), tensor: 4 (over x), context: 32 (over z_hi, y, core).
Axes of the slice: x: 4, y: 8, z: 8 (z_hi: 2, z_lo: 4; z = z_hi * 4 + z_lo), core: 2. Of those that a mesh axis runs over, the one named last changes fastest.
Arguments:
- inputs: bfloat16 [4, 4096, 4096], P('dp', 'tensor', 'context'), may hold values from -6 to 6
- out_grad: bfloat16 [4, 4096, 4096], P('dp', 'tensor', 'context'), may hold values from -6 to 6
- filters: float32 [256, 4096], P('tensor', 'context'), may hold values from -0.09375 to 0.09375
- skip: float32 [4096], P('tensor'), may hold values from 0.5 to 1.5
Outputs:
- grad_input: bfloat16 [4, 4096, 4096], P('dp', 'tensor', 'context')
- grad_filter: float32 [256, 4096], P('tensor', 'context')
All inputs are finite; a program needn't handle non-finite values.
Results may differ from a plain program's by a relative error of at most 0.0034.
Values may be sent and summed in bfloat16 or wider, within the bound.
A program may use at most 64 MiB of HBM per device.

v0:
```python
import math

import jax
import jax.numpy as jnp
from jax import lax
from jax.sharding import Mesh
from jax.sharding import PartitionSpec as P

GROUP = 16
CONTEXT = ("context_0", "context_1", "context_2")


exact_mode = lax.Precision.HIGHEST


def in_one_piece(arrays, axis, split_dim, concat_dim, along):
    widths = [a.shape[along] for a in arrays]
    both = jnp.concatenate(arrays, axis=along)
    whole = lax.all_to_all(both, axis, split_axis=split_dim, concat_axis=concat_dim, tiled=True)
    return tuple(jnp.split(whole, [sum(widths[:k]) for k in range(1, len(widths))], axis=along))


def cut_along(value, dim, devices):
    lengths = value.shape
    pieces = value.reshape(*lengths[:dim], devices, lengths[dim] // devices, *lengths[dim + 1 :])
    return jnp.moveaxis(pieces, dim, 0)


def joined_along(pieces, dim):
    pieces = jnp.moveaxis(pieces, 0, dim)
    lengths = pieces.shape
    return pieces.reshape(*lengths[:dim], lengths[dim] * lengths[dim + 1], *lengths[dim + 2 :])


def moved_by_axis(pieces, axes, turns):
    inside = pieces.shape[1:]
    whole = pieces.reshape(*(lax.axis_size(a) for a in axes), *inside)
    for k in turns:
        whole = lax.all_to_all(whole, axes[k], k, k, tiled=True)
    return whole.reshape(-1, *inside)


def two_step_exchange(value, groups, turns, split_dim, concat_dim):
    devices = lax.axis_size(groups[0]) * lax.axis_size(groups[1])
    pieces = cut_along(value, split_dim, devices)
    return joined_along(moved_by_axis(pieces, groups, turns), concat_dim)


def total_of_pieces(value, axis):
    return lax.all_gather(value, axis).sum(0)


def dft_tables(size_one, size_two):
    padded_len = size_one * size_two
    range_one = jnp.arange(size_one, dtype=jnp.int32)
    range_two = jnp.arange(size_two, dtype=jnp.int32)
    angle_one = (range_one[:, None] * range_one[None, :] % size_one).astype(jnp.float32) * (
        -2.0 * math.pi / size_one
    )
    angle_two = (range_two[:, None] * range_two[None, :] % size_two).astype(jnp.float32) * (
        -2.0 * math.pi / size_two
    )
    angle_turn = (range_one[:, None] * range_two[None, :] % padded_len).astype(jnp.float32) * (
        -2.0 * math.pi / padded_len
    )
    return (
        jnp.cos(angle_one),
        jnp.sin(angle_one),
        jnp.cos(angle_two),
        jnp.sin(angle_two),
        jnp.cos(angle_turn),
        jnp.sin(angle_turn),
    )


def left_mul(matrix, operand):
    return jnp.einsum("kj,mjl->mkl", matrix, operand, precision=exact_mode)


def right_mul(operand, matrix):
    return jnp.einsum("mkj,jl->mkl", operand, matrix, precision=exact_mode)


def forward_real(signal, tables):
    one_re, one_im, two_re, two_im, turn_re, turn_im = tables
    half_rows = signal.shape[1]
    step_re = left_mul(one_re[:, :half_rows], signal)
    step_im = left_mul(one_im[:, :half_rows], signal)
    mid_re = step_re * turn_re - step_im * turn_im
    mid_im = step_re * turn_im + step_im * turn_re
    spec_re = right_mul(mid_re, two_re) - right_mul(mid_im, two_im)
    spec_im = right_mul(mid_re, two_im) + right_mul(mid_im, two_re)
    return (spec_re, spec_im)


def inverse_real(spec_re, spec_im, tables, half_rows):
    one_re, one_im, two_re, two_im, turn_re, turn_im = tables
    back_re = right_mul(spec_re, two_re) + right_mul(spec_im, two_im)
    back_im = right_mul(spec_im, two_re) - right_mul(spec_re, two_im)
    mid_re = back_re * turn_re + back_im * turn_im
    mid_im = back_im * turn_re - back_re * turn_im
    padded_len = one_re.shape[0] * two_re.shape[0]
    return (
        left_mul(one_re[:half_rows], mid_re) + left_mul(one_im[:half_rows], mid_im)
    ) / padded_len


def owner_groups(owners, own_ch, own_grp):
    starts = jnp.arange(owners, dtype=jnp.int32)[:, None] * own_ch // GROUP
    return starts + jnp.arange(own_grp, dtype=jnp.int32)[None, :]


def per_device(inputs, out_grad, filters, skip):
    tok_dev = inputs.shape[2]
    ch_dev = inputs.shape[1]
    grp_dev = filters.shape[0]
    owners = lax.axis_size(CONTEXT)
    seq_len = tok_dev * owners
    padded_len = 2 * seq_len
    own_ch = ch_dev // owners
    own_grp = max(1, own_ch // GROUP)
    per_group = own_ch // own_grp
    size_one = 1 << (padded_len.bit_length() - 1) // 2
    while padded_len % size_one != 0:
        size_one = size_one // 2
    size_two = padded_len // size_one
    half_rows = size_one // 2
    tables = dft_tables(size_one, size_two)
    moved_in, moved_grad = in_one_piece((inputs, out_grad), CONTEXT, 1, 2, 0)
    slot_groups = owner_groups(owners, own_ch, own_grp)
    pick_rows = (
        slot_groups[:, :, None] == jnp.arange(grp_dev, dtype=jnp.int32)[None, None, :]
    ).astype(jnp.float32)
    outgoing = jnp.einsum("ojg,gt->ojt", pick_rows, filters, precision=exact_mode)
    own_filter = lax.all_to_all(outgoing, CONTEXT, split_axis=0, concat_axis=2, tiled=True).reshape(
        own_grp, seq_len
    )
    sig_in = moved_in[0].astype(jnp.float32).reshape(own_ch, half_rows, size_two)
    sig_grad = moved_grad[0].astype(jnp.float32).reshape(own_ch, half_rows, size_two)
    in_re, in_im = forward_real(sig_in, tables)
    grad_re, grad_im = forward_real(sig_grad, tables)
    filt_re, filt_im = forward_real(own_filter.reshape(own_grp, half_rows, size_two), tables)
    grad_re4 = grad_re.reshape(own_grp, per_group, size_one, size_two)
    grad_im4 = grad_im.reshape(own_grp, per_group, size_one, size_two)
    filt_re4 = filt_re[:, None]
    filt_im4 = filt_im[:, None]
    prod_re = (filt_re4 * grad_re4 + filt_im4 * grad_im4).reshape(own_ch, size_one, size_two)
    prod_im = (filt_re4 * grad_im4 - filt_im4 * grad_re4).reshape(own_ch, size_one, size_two)
    correlated = (
        inverse_real(prod_re, prod_im, tables, half_rows)
        .reshape(1, own_ch, seq_len)
        .astype(jnp.bfloat16)
    )
    returned = two_step_exchange(
        correlated, (("context_0", "context_1"), "context_2"), (1, 0), 2, 1
    )
    grad_input = (
        returned.astype(jnp.float32) + skip[None, :, None] * out_grad.astype(jnp.float32)
    ).astype(jnp.bfloat16)
    in_re4 = in_re.reshape(own_grp, per_group, size_one, size_two)
    in_im4 = in_im.reshape(own_grp, per_group, size_one, size_two)
    lag_re = (in_re4 * grad_re4 + in_im4 * grad_im4).sum(axis=1)
    lag_im = (in_re4 * grad_im4 - in_im4 * grad_re4).sum(axis=1)
    own_terms = inverse_real(lag_re, lag_im, tables, half_rows).reshape(own_grp, seq_len)
    pieces = lax.all_to_all(
        own_terms.reshape(own_grp, owners, tok_dev),
        CONTEXT,
        split_axis=1,
        concat_axis=0,
        tiled=True,
    )
    row_groups = owner_groups(owners, own_ch, own_grp).reshape(-1)
    pick_sum = (jnp.arange(grp_dev, dtype=jnp.int32)[:, None] == row_groups[None, :]).astype(
        jnp.float32
    )
    local_sum = jnp.dot(pick_sum, pieces.reshape(owners * own_grp, tok_dev), precision=exact_mode)
    summed = total_of_pieces(local_sum, "dp")
    norm_scale = 1.0 / math.sqrt(lax.axis_size("dp") * GROUP * seq_len)
    return (grad_input, summed * norm_scale)


def solution(mesh):
    split = Mesh(
        mesh.devices.reshape(mesh.shape["dp"], mesh.shape["tensor"], 2, 8, 2),
        ("dp", "tensor", "context_0", "context_1", "context_2"),
    )
    placed = (
        P("dp", "tensor", CONTEXT),
        P("dp", "tensor", CONTEXT),
        P("tensor", CONTEXT),
        P("tensor"),
    )
    return jax.shard_map(
        per_device,
        mesh=split,
        in_specs=placed,
        out_specs=(P("dp", "tensor", CONTEXT), P("tensor", CONTEXT)),
        check_vma=False,
    )
```

profile of v0, /device:TPU:20, one launch (start us, length us, event | category | flops | bytes accessed | tf_op | source)
XLA Modules:
  0.0 128.3 jit_solution(11315829979133608600)
XLA Ops:
  0.8 0.6 copy-done
  1.6 0.6 copy.35
  2.2 16.0 %all-to-all-start = ((f32[32,2,128]{2,1,0:T(2,128)}), f32[32,2,128]{2,1,0:T(2,128)S(1)}, u32[]{:S(2)}, u32[]{:S(2)}) async-start(f32[32,2,128]{2,1,0:T(2,128)} %copy.35), calls=%async_computation | async-start | bytes 65536 | tf_op jit(solution)/shard_map/all_to_all | solution.py:135
  18.6 0.4 copy.38
  19.0 0.5 copy-done.9
  19.6 0.4 copy.37
  20.0 2.0 %pad_maximum_fusion = bf16[2,1024,128]{2,0,1:T(2,128)(2,1)} fusion(bf16[1,1024,128]{2,0,1:T(2,128)(2,1)S(1)} %copy.38, bf16[1,1024,128]{2,0,1:T(2,128)(2,1)S(1)} %copy.37), kind=kLoop, calls=%fused_computation.43 | loop fusion | flops 1048576 | bytes 1048576 | tf_op jit(solution)/shard_map/concatenate | solution.py:18
  22.1 6.6 %all-to-all-done = f32[32,2,128]{2,1,0:T(2,128)S(1)} async-done(((f32[32,2,128]{2,1,0:T(2,128)}), f32[32,2,128]{2,1,0:T(2,128)S(1)}, u32[]{:S(2)}, u32[]{:S(2)}) %all-to-all-start) | async-done | bytes 32800 | tf_op jit(solution)/shard_map/all_to_all | solution.py:135
  28.7 6.1 %all-to-all-start.1 = ((bf16[2,1024,128]{2,0,1:T(2,128)(2,1)}), bf16[2,1024,128]{2,0,1:T(2,128)(2,1)S(1)}, u32[]{:S(2)}, u32[]{:S(2)}) async-start(bf16[2,1024,128]{2,0,1:T(2,128)(2,1)} %pad_maximum_fusion), calls=%async_computation.1 | async-start | bytes 1048576 | tf_op jit(solution)/shard_map/all_to_all | solution.py:19
  35.3 0.5 fusion.32
  35.8 0.5 fusion.49
  36.2 1.1 convolution_add_fusion.5
  37.3 1.1 convolution_subtract_fusion.4
  38.4 16.3 %all-to-all-done.1 = bf16[2,1024,128]{2,0,1:T(2,128)(2,1)S(1)} async-done(((bf16[2,1024,128]{2,0,1:T(2,128)(2,1)}), bf16[2,1024,128]{2,0,1:T(2,128)(2,1)S(1)}, u32[]{:S(2)}, u32[]{:S(2)}) %all-to-all-start.1) | async-done | bytes 524320 | tf_op jit(solution)/shard_map/all_to_all | solution.py:19
  54.7 0.3 copy.68
  55.0 0.6 convolution_bitcast_fusion.2
  55.6 0.6 convolution_bitcast_fusion.3
  56.3 1.3 fusion.18
  57.5 1.2 fusion.19
  58.8 0.6 convolution_bitcast_fusion
  59.4 0.6 convolution_bitcast_fusion.1
  60.0 2.2 %fusion.21 = f32[32,64,128]{2,1,0:T(8,128)} fusion(f32[32,64,128]{2,1,0:T(8,128)S(1)} %convolution_bitcast_fusion, f32[32,64,128]{2,1,0:T(8,128)S(1)} %convolution_bitcast_fusion.1, f32[64,128]{1,0:T(8,128)S(1)} %get-tuple-element.7, f32[64,128]{1,0:T(8,128)S(1)} %get-tuple-element.8), kind=kOutput, calls=%fused_computation.54 | convolution fusion | flops 403668992 | bytes 3211264 | tf_op jit(solution)/shard_map/mkj,jl->mkl/dot_general | solution.py:81
  62.2 2.2 %fusion.20 = f32[32,64,128]{2,1,0:T(8,128)} fusion(f32[32,64,128]{2,1,0:T(8,128)S(1)} %convolution_bitcast_fusion, f32[32,64,128]{2,1,0:T(8,128)S(1)} %convolution_bitcast_fusion.1, f32[64,128]{1,0:T(8,128)S(1)} %get-tuple-element.7, f32[64,128]{1,0:T(8,128)S(1)} %get-tuple-element.8), kind=kOutput, calls=%fused_computation.53 | convolution fusion | flops 403668992 | bytes 3211264 | tf_op jit(solution)/shard_map/mkj,jl->mkl/dot_general | solution.py:81
  64.5 1.2 convolution_add_fusion.2
  65.7 2.4 %fusion.4 = (f32[32,64,128]{2,1,0:T(8,128)S(1)}, f32[32,64,128]{2,1,0:T(8,128)S(1)}, f32[32,64,128]{2,1,0:T(8,128)}) fusion(f32[32,64,128]{2,1,0:T(8,128)S(1)} %convolution_add_fusion.2, f32[2,64,128]{2,1,0:T(8,128)S(1)} %copy-done.7, f32[2,64,128]{2,1,0:T(8,128)S(1)} %copy-done.8, f32[32,64,128]{2,1,0:T(8,128)S(1)} %fusion.19, ...), kind=kOutput, calls=%fused_computation.26 | convolution fusion | flops 405504000 | bytes 7536640 | tf_op jit(solution)/shard_map/mkj,jl->mkl/dot_general | solution.py:81
  68.2 1.5 %fusion.42 = f32[32,64,128]{2,1,0:T(8,128)S(1)} fusion(f32[32,64,128]{2,1,0:T(8,128)S(1)} %get-tuple-element.5), kind=kOutput, calls=%fused_computation.80 | convolution fusion | flops 402882560 | bytes 2097152 | tf_op jit(solution)/shard_map/mkj,jl->mkl/dot_general | solution.py:81
  69.6 1.2 fusion.44
  70.9 1.2 convolution_subtract_fusion.1
  72.1 1.2 convolution_add_fusion.1
  73.4 0.9 fusion.9
  74.2 0.9 fusion.1
  75.1 0.7 copy.43
  75.8 4.1 %all-to-all-start.2 = ((bf16[16,2,1,32,128]{4,0,3,2,1:T(8,128)(2,1)}), bf16[16,2,1,32,128]{4,0,3,2,1:T(8,128)(2,1)}, u32[]{:S(2)}, u32[]{:S(2)}) async-start(bf16[16,2,1,32,128]{4,0,3,2,1:T(8,128)(2,1)} %copy.43), calls=%async_computation.2 | async-start | bytes 524288 | tf_op jit(solution)/shard_map/all_to_all | solution.py:39
  80.0 2.6 %convolution_subtract_fusion = f32[32,64,128]{2,1,0:T(8,128)S(1)} fusion(f32[32,64,128]{2,1,0:T(8,128)} %fusion.21, f32[32,64,128]{2,1,0:T(8,128)S(1)} %convolution_bitcast_fusion, f32[32,64,128]{2,1,0:T(8,128)S(1)} %convolution_bitcast_fusion.1, f32[64,128]{1,0:T(8,128)S(1)} %get-tuple-element.7, f32[64,128]{1,0:T(8,128)S(1)} %get-tuple-element.8), kind=kOutput, calls=%fused_computation.5 | convolution fusion | flops 403931136 | bytes 4259840 | tf_op jit(solution)/shard_map/mkj,jl->mkl/dot_general | solution.py:81
  82.6 1.5 %bitcast_reduce_fusion.1 = (f32[2,64,128]{2,1,0:T(8,128)S(1)}, f32[2,64,128]{2,1,0:T(8,128)S(1)}) fusion(f32[32,64,128]{2,1,0:T(8,128)S(1)} %convolution_add_fusion.2, f32[32,64,128]{2,1,0:T(8,128)S(1)} %convolution_subtract_fusion, f32[32,64,128]{2,1,0:T(8,128)S(1)} %copy-done.2, f32[32,64,128]{2,1,0:T(8,128)S(1)} %copy-done.1, ...), kind=kOutput, calls=%fused_computation.29 | convolution fusion | flops 405995520 | bytes 6488064 | tf_op jit(solution)/shard_map/mkj,jl->mkl/dot_general | solution.py:81
  84.1 0.5 fusion.36
  84.6 0.5 fusion.38
  85.0 0.5 convolution_subtract_fusion.3
  85.5 0.5 convolution_add_fusion.4
  86.7 0.6 copy.48
  87.4 6.1 %all-to-all-start.4 = ((f32[2,32,128]{2,0,1:T(2,128)}), f32[2,32,128]{2,0,1:T(2,128)S(1)}, u32[]{:S(2)}, u32[]{:S(2)}) async-start(f32[2,32,128]{2,0,1:T(2,128)} %copy.48), calls=%async_computation.4 | async-start | bytes 65536 | tf_op jit(solution)/shard_map/all_to_all | solution.py:165
  93.6 1.9 %copy.44 = bf16[16,2,1,32,128]{4,1,3,2,0:T(2,128)(2,1)} copy(bf16[16,2,1,32,128]{4,0,3,2,1:T(8,128)(2,1)} %all-to-all-done.2) | data formatting | bytes 524288 | tf_op jit(solution)/shard_map/all_to_all | solution.py:39
  95.6 8.4 %all-to-all-done.4 = f32[2,32,128]{2,0,1:T(2,128)S(1)} async-done(((f32[2,32,128]{2,0,1:T(2,128)}), f32[2,32,128]{2,0,1:T(2,128)S(1)}, u32[]{:S(2)}, u32[]{:S(2)}) %all-to-all-start.4) | async-done | bytes 32800 | tf_op jit(solution)/shard_map/all_to_all | solution.py:165
  104.0 5.7 %all-to-all-start.3 = ((bf16[16,2,1,32,128]{4,1,3,2,0:T(2,128)(2,1)}), bf16[16,2,1,32,128]{4,1,3,2,0:T(2,128)(2,1)S(1)}, u32[]{:S(2)}, u32[]{:S(2)}) async-start(bf16[16,2,1,32,128]{4,1,3,2,0:T(2,128)(2,1)} %copy.44), calls=%async_computation.3 | async-start | bytes 524288 | tf_op jit(solution)/shard_map/all_to_all | solution.py:39
  109.8 16.3 %all-gather = f32[256,128]{1,0:T(8,128)S(1)} all-gather(f32[64,128]{1,0:T(8,128)S(1)} %fusion.103), channel_id=2, replica_groups=mesh['dp'=4,'tensor'=4,'context_0'=2,'context_1'=8,'context_2'=2] {'dp'}, dimensions={0}, use_global_device_ids=true | all-gather | bytes 163840 | tf_op jit(solution)/shard_map/all_gather | solution.py:50
  126.1 0.6 broadcast_multiply_fusion
  126.8 0.6 copy-done.10
  127.4 0.9 fusion.13
  (36 shorter events, 2.4 us)
Async XLA Ops:
  0.6 0.8 copy-start
  0.6 17.9 %copy-start.3 = (bf16[1,1024,128]{2,1,0:T(8,128)(2,1)S(1)}, bf16[1,1024,128]{2,1,0:T(8,128)(2,1)}, u32[]{:S(2)}) copy-start(bf16[1,1024,128]{2,1,0:T(8,128)(2,1)} %param.5) | copy-start | bytes 786436
  2.2 26.4 %all-to-all-start = ((f32[32,2,128]{2,1,0:T(2,128)}), f32[32,2,128]{2,1,0:T(2,128)S(1)}, u32[]{:S(2)}, u32[]{:S(2)}) async-start(f32[32,2,128]{2,1,0:T(2,128)} %copy.35), calls=%async_computation | async-start | bytes 65536 | tf_op jit(solution)/shard_map/all_to_all | solution.py:135
  18.6 1.0 copy-start.9
  22.1 37.3 %copy-start.4 = (f32[64,64]{0,1:T(8,128)}, f32[64,64]{0,1:T(8,128)S(1)}, u32[]{:S(2)}) copy-start(f32[64,64]{0,1:T(8,128)S(1)} %fusion.110) | copy-start | bytes 49156
  28.7 26.0 %all-to-all-start.1 = ((bf16[2,1024,128]{2,0,1:T(2,128)(2,1)}), bf16[2,1024,128]{2,0,1:T(2,128)(2,1)S(1)}, u32[]{:S(2)}, u32[]{:S(2)}) async-start(bf16[2,1024,128]{2,0,1:T(2,128)(2,1)} %pad_maximum_fusion), calls=%async_computation.1 | async-start | bytes 1048576 | tf_op jit(solution)/shard_map/all_to_all | solution.py:19
  64.5 1.3 copy-start.7
  64.5 1.3 copy-start.8
  72.1 1.2 copy-start.5
  75.8 11.6 %all-to-all-start.2 = ((bf16[16,2,1,32,128]{4,0,3,2,1:T(8,128)(2,1)}), bf16[16,2,1,32,128]{4,0,3,2,1:T(8,128)(2,1)}, u32[]{:S(2)}, u32[]{:S(2)}) async-start(bf16[16,2,1,32,128]{4,0,3,2,1:T(8,128)(2,1)} %copy.43), calls=%async_computation.2 | async-start | bytes 524288 | tf_op jit(solution)/shard_map/all_to_all | solution.py:39
  79.9 2.6 %copy-start.1 = (f32[32,64,128]{2,1,0:T(8,128)S(1)}, f32[32,64,128]{2,1,0:T(8,128)}, u32[]{:S(2)}) copy-start(f32[32,64,128]{2,1,0:T(8,128)} %fusion.20) | copy-start | bytes 3145732
  79.9 2.6 %copy-start.2 = (f32[32,64,128]{2,1,0:T(8,128)S(1)}, f32[32,64,128]{2,1,0:T(8,128)}, u32[]{:S(2)}) copy-start(f32[32,64,128]{2,1,0:T(8,128)} %get-tuple-element.6) | copy-start | bytes 3145732
  85.5 0.8 copy-start.6
  87.4 16.6 %all-to-all-start.4 = ((f32[2,32,128]{2,0,1:T(2,128)}), f32[2,32,128]{2,0,1:T(2,128)S(1)}, u32[]{:S(2)}, u32[]{:S(2)}) async-start(f32[2,32,128]{2,0,1:T(2,128)} %copy.48), calls=%async_computation.4 | async-start | bytes 65536 | tf_op jit(solution)/shard_map/all_to_all | solution.py:165
  104.0 22.7 %all-to-all-start.3 = ((bf16[16,2,1,32,128]{4,1,3,2,0:T(2,128)(2,1)}), bf16[16,2,1,32,128]{4,1,3,2,0:T(2,128)(2,1)S(1)}, u32[]{:S(2)}, u32[]{:S(2)}) async-start(bf16[16,2,1,32,128]{4,1,3,2,0:T(2,128)(2,1)} %copy.44), calls=%async_computation.3 | async-start | bytes 524288 | tf_op jit(solution)/shard_map/all_to_all | solution.py:39
  126.7 0.7 copy-start.10
where the time goes:
time: 129 us; the launch traced here: 128 us
  starting transfers between devices  38.1 us (30%)
  waiting for transfers between devices  31.3 us (24%)
  matrix products  30.2 us (23%)
  blocking collectives  16.3 us (13%)
  local copies, waits for them, and re-layouts  7.39 us (6%)
  other arithmetic  4.03 us (3%)
    dot_general x20, matrix products, right_mul(): return jnp.einsum('mkj,jl->mkl', operand, matrix, precision=exact_mode)  24.8 us
    all_gather x1, blocking collectives, total_of_pieces(): return lax.all_gather(value, axis).sum(0)  16.3 us
    all_to_all x1, waiting for transfers between devices, in_one_piece(): lax.all_to_all(both, axis, split_axis=split_dim, concat_axis=concat_dim,...  16.3 us
    all_to_all x1, starting transfers between devices, per_device(): lax.all_to_all(outgoing, CONTEXT, split_axis=0, concat_axis=2, tiled=True)  16 us
    all_to_all x2, starting transfers between devices, moved_by_axis(): whole = lax.all_to_all(whole, axes[k], k, k, tiled=True)  9.8 us
    all_to_all x1, waiting for transfers between devices, per_device(): lax.all_to_all(own_terms.reshape(own_grp, owners, tok_dev), CONTEXT, spli...  8.44 us
    all_to_all x1, waiting for transfers between devices, per_device(): lax.all_to_all(outgoing, CONTEXT, split_axis=0, concat_axis=2, tiled=True)  6.58 us
    all_to_all x1, starting transfers between devices, per_device(): lax.all_to_all(own_terms.reshape(own_grp, owners, tok_dev), CONTEXT, spli...  6.14 us
  transfers between devices with their start and end apart: 5, of which 3 were waited for; matrix products, arithmetic and copies ran while one was open for 13% of the time, Pallas kernels for 0%

commit v1 on v0

v1 whole, which is shorter than its diff:
```python
import functools
import math

import jax
import jax.numpy as jnp
from jax import lax
from jax.experimental import pallas as pl
from jax.experimental.pallas import tpu as pltpu
from jax.sharding import PartitionSpec as P

GROUP = 16
LANES = 128
MESH = pl.DeviceIdType.MESH
F32 = jnp.float32
BF16 = jnp.bfloat16


def whole_wait(ref, sem):
    pltpu.make_async_copy(ref, ref, sem).wait()


def shift_table(taps, pad):
    width = taps.shape[1] + pad
    rows = jnp.concatenate([taps, jnp.zeros((16, pad), F32)], axis=1)
    row = lax.broadcasted_iota(jnp.int32, (16, width), 0)
    for bit in (1, 2, 4, 8):
        rows = jnp.where(row % (2 * bit) >= bit, pltpu.roll(rows, bit, 1), rows)
    return rows


def kernel(sizes, x_in, g_in, f_in, s_in, gi_out, gf_out,
           f_send, f_all, g_all, x_all, toe_hi, toe_lo, acc, back, back_all,
           direct, lag_rows, lag_send, lag_all, g_here,
           s_send, s_recv, s_loc):
    owners, seqs, own_grp, scale = sizes
    blocks = owners // 2
    taps = owners * LANES
    me = lax.axis_index("context")
    seq = lax.axis_index("dp")
    core, place = me % 2, me // 2
    half = owners // 2

    def peer(k):
        v = (k + half) % owners + k // half
        far = (me // half + v // half) % 2
        near = (me % half // 2 + v % half // 2) % (half // 2)
        return far * half + near * 2 + (core + v) % 2

    def to_peers(body):
        def step(k, carry):
            body(peer(k))
            return carry

        lax.fori_loop(0, owners - 1, step, 0)

    barrier = pltpu.get_barrier_semaphore()
    to_peers(lambda o: pl.semaphore_signal(
        barrier, inc=1, device_id={"context": o}, device_id_type=MESH))
    for r in range(1, seqs):
        pl.semaphore_signal(
            barrier, inc=1, device_id={"dp": (seq + r) % seqs}, device_id_type=MESH)

    here = pltpu.make_async_copy(g_in, g_here, s_loc.at[0])
    here.start()
    for o in range(owners):
        f_send[o] = f_in[own_grp * o : own_grp * (o + 1), :]
    f_all[pl.ds(me, 1)] = f_send[pl.ds(me, 1)]
    g_all[:, :, blocks:] = jnp.zeros((2, own_grp, blocks, GROUP, LANES), BF16)

    mine = pl.ds(own_grp * me, own_grp)
    pltpu.make_async_copy(g_in.at[mine], g_all.at[core, :, place], s_recv.at[1]).start()
    pltpu.make_async_copy(x_in.at[mine], x_all.at[core, :, place], s_recv.at[2]).start()

    pl.semaphore_wait(barrier, owners - 1 + seqs - 1)

    def send(src, dst, k, where):
        pltpu.make_async_remote_copy(
            src_ref=src, dst_ref=dst, send_sem=s_send.at[k], recv_sem=s_recv.at[k],
            device_id=where, device_id_type=MESH).start()

    to_peers(lambda o: send(f_send.at[o], f_all.at[me], 0, {"context": o}))
    to_peers(lambda o: send(
        g_in.at[pl.ds(own_grp * o, own_grp)], g_all.at[core, :, place], 1, {"context": o}))
    to_peers(lambda o: send(
        x_in.at[pl.ds(own_grp * o, own_grp)], x_all.at[core, :, place], 2, {"context": o}))

    here.wait()
    by_row = s_in[...].T
    per = LANES // GROUP
    for m in range(s_in.shape[0]):
        part = g_here[per * m : per * (m + 1)].reshape(LANES, LANES).astype(F32)
        part = part * jnp.broadcast_to(by_row[:, m : m + 1], (LANES, LANES))
        direct[per * m : per * (m + 1)] = part.reshape(per, GROUP, LANES)

    whole_wait(f_all.at[pl.ds(0, owners - 1)], s_recv.at[0])
    for g in range(own_grp):
        lead = jnp.zeros((LANES, LANES), BF16)
        toe_hi[g, :, 0:LANES] = lead
        toe_lo[g, :, 0:LANES] = lead
        wide = jnp.concatenate(
            [jnp.broadcast_to(f_all[j, g : g + 1, :], (16, LANES)) for j in range(owners)],
            axis=1)
        rows = shift_table(wide, LANES)
        for q in range(LANES // 16):
            moved = rows if q == 0 else pltpu.roll(rows, 16 * q, 1)
            moved = moved[:, :taps]
            high = moved.astype(BF16)
            toe_hi[g, 16 * q : 16 * (q + 1), LANES:] = high
            toe_lo[g, 16 * q : 16 * (q + 1), LANES:] = (moved - high.astype(F32)).astype(BF16)

    def rows_of(ref, g, start, count):
        return jnp.concatenate(
            [ref[c, g, start : start + count].reshape(count * GROUP, LANES) for c in range(2)],
            axis=1)

    whole_wait(x_all, s_recv.at[1])
    step = min(4, blocks)
    for g in range(own_grp):
        for e in range(0, blocks, step):
            count = blocks - e
            left = jnp.concatenate(
                [rows_of(g_all, g, e + t, count) for t in range(step)], axis=1)
            lo, hi = 2 * LANES * e, 2 * LANES * (e + step)
            total = None
            for toe in (toe_lo, toe_hi):
                right = jnp.concatenate(
                    [toe[g, :, LANES + lo : LANES + hi], toe[g, :, lo:hi]], axis=0)
                term = lax.dot_general(
                    left, right, (((1,), (1,)), ((), ())), preferred_element_type=F32)
                total = term if total is None else total + term
            if e == 0:
                acc[...] = total
            else:
                acc[0 : count * GROUP] += total
        for c in range(2):
            back[c, g] = acc[:, LANES * c : LANES * (c + 1)].astype(BF16).reshape(
                blocks, GROUP, LANES)
        pltpu.make_async_copy(
            back.at[core, g, place], back_all.at[own_grp * me + g], s_recv.at[3]).start()
        to_peers(lambda o: send(
            back.at[o % 2, g, o // 2], back_all.at[own_grp * me + g], 3, {"context": o}))

    whole_wait(x_all, s_recv.at[2])
    for g in range(own_grp):
        turned = jnp.concatenate(
            [x_all[c, g].reshape(blocks * GROUP, LANES).T for c in range(2)], axis=0)
        carry = jnp.zeros((LANES, LANES), F32)
        for d in reversed(range(blocks)):
            square = jnp.dot(
                turned, rows_of(g_all, g, d, blocks), preferred_element_type=F32)
            at = 2 * LANES * d
            lag_rows[:, at : at + LANES] = square[:LANES, :LANES] + square[LANES:, LANES:]
            lag_rows[:, at + LANES : at + 2 * LANES] = square[:LANES, LANES:] + carry
            carry = square[LANES:, :LANES]
        width = taps + LANES
        total = None
        for q in reversed(range(LANES // 8)):
            row = jnp.concatenate(
                [jnp.zeros((8, LANES), F32), lag_rows[8 * q : 8 * (q + 1), :]], axis=1)
            total = row if total is None else row + pltpu.roll(total, width - 8, 1)
        row = lax.broadcasted_iota(jnp.int32, (8, width), 0)
        for bit in (1, 2, 4):
            total = jnp.where(
                row % (2 * bit) >= bit, pltpu.roll(total, width - bit, 1), total)
        line = jnp.sum(total, axis=0, keepdims=True)[:, LANES:]
        for j in range(owners):
            lag_send[j, g : g + 1, :] = line[:, LANES * j : LANES * (j + 1)]

    pltpu.make_async_copy(lag_send.at[me], lag_all.at[seq, me], s_recv.at[4]).start()
    to_peers(lambda o: send(lag_send.at[o], lag_all.at[seq, me], 4, {"context": o}))
    whole_wait(lag_all.at[0], s_recv.at[4])
    for r in range(1, seqs):
        send(lag_all.at[seq], lag_all.at[seq], 5, {"dp": (seq + r) % seqs})

    whole_wait(back_all, s_recv.at[3])
    gi_out[...] = (back_all[...].astype(F32) + direct[...]).astype(BF16)

    whole_wait(lag_all.at[pl.ds(0, seqs - 1)], s_recv.at[5])
    summed = lag_all[0]
    for b in range(1, seqs):
        summed = summed + lag_all[b]
    summed = summed * scale
    for o in range(owners):
        gf_out[own_grp * o : own_grp * (o + 1), :] = summed[o]

    others = own_grp * (owners - 1)
    whole_wait(f_send.at[pl.ds(0, owners - 1)], s_send.at[0])
    whole_wait(g_in.at[pl.ds(0, others)], s_send.at[1])
    whole_wait(x_in.at[pl.ds(0, others)], s_send.at[2])
    whole_wait(back_all.at[pl.ds(0, others)], s_send.at[3])
    whole_wait(lag_send.at[pl.ds(0, owners - 1)], s_send.at[4])
    whole_wait(lag_all.at[pl.ds(0, seqs - 1)], s_send.at[5])


def per_device(inputs, out_grad, filters, skip):
    channels, tok = inputs.shape[1], inputs.shape[2]
    groups = filters.shape[0]
    owners, seqs = lax.axis_size("context"), lax.axis_size("dp")
    own_grp = groups // owners
    blocks = owners // 2
    scale = 1.0 / math.sqrt(seqs * GROUP * tok * owners)
    vmem = pl.BlockSpec(memory_space=pltpu.VMEM)
    anywhere = pl.BlockSpec(memory_space=pl.ANY)
    tiles = (groups, GROUP, LANES)
    held = (2, own_grp, blocks, GROUP, LANES)
    grad_input, grad_filter = pl.pallas_call(
        functools.partial(kernel, (owners, seqs, own_grp, scale)),
        out_shape=(
            jax.ShapeDtypeStruct(tiles, BF16),
            jax.ShapeDtypeStruct((groups, LANES), F32),
        ),
        in_specs=[anywhere, anywhere, vmem, vmem],
        out_specs=(vmem, vmem),
        scratch_shapes=[
            pltpu.VMEM((owners, own_grp, LANES), F32),
            pltpu.VMEM((owners, own_grp, LANES), F32),
            pltpu.VMEM((2, own_grp, 2 * blocks, GROUP, LANES), BF16),
            pltpu.VMEM(held, BF16),
            pltpu.VMEM((own_grp, LANES, LANES * (owners + 1)), BF16),
            pltpu.VMEM((own_grp, LANES, LANES * (owners + 1)), BF16),
            pltpu.VMEM((blocks * GROUP, 2 * LANES), F32),
            pltpu.VMEM(held, BF16),
            pltpu.VMEM(tiles, BF16),
            pltpu.VMEM(tiles, F32),
            pltpu.VMEM((LANES, LANES * owners), F32),
            pltpu.VMEM((owners, own_grp, LANES), F32),
            pltpu.VMEM((seqs, owners, own_grp, LANES), F32),
            pltpu.VMEM(tiles, BF16),
            pltpu.SemaphoreType.DMA((6,)),
            pltpu.SemaphoreType.DMA((6,)),
            pltpu.SemaphoreType.DMA((1,)),
        ],
        compiler_params=pltpu.CompilerParams(
            collective_id=0, has_side_effects=True, vmem_limit_bytes=48 * 1024 * 1024),
    )(
        inputs.reshape(tiles),
        out_grad.reshape(tiles),
        filters,
        skip.reshape(channels // LANES, LANES),
    )
    return grad_input.reshape(1, channels, tok), grad_filter


def solution(mesh):
    placed = (
        P("dp", "tensor", "context"),
        P("dp", "tensor", "context"),
        P("tensor", "context"),
        P("tensor"),
    )
    return jax.shard_map(
        per_device,
        mesh=mesh,
        in_specs=placed,
        out_specs=(P("dp", "tensor", "context"), P("tensor", "context")),
        check_vma=False,
    )
```

time: 129 us -> 57.4 us (0.44)
  the two profiles are of different devices: /device:TPU:20 before, /device:TPU:1 now
where the time goes in v1:
time: 57.4 us; the launch traced here: 57 us
  Pallas kernels  51.7 us (90%)
  local copies, waits for them, and re-layouts  4.66 us (8%)
  between operations  0.65 us (1%)
    pallas_call x1, Pallas kernels, per_device(): pl.pallas_call(functools.partial(kernel, (owners, seqs, own_grp, scale)),...  51.7 us
    unnamed x10, local copies, waits for them, and re-layouts  4.66 us

profile of v1, /device:TPU:1, one launch (start us, length us, event | category | flops | bytes accessed | tf_op | source)
XLA Modules:
  0.0 57.0 jit_solution(10453341584410343442)
XLA Ops:
  0.6 0.0 copy-start.3
  0.6 0.7 %copy-done.3 = f32[1024]{0:T(1024)S(1)} copy-done((f32[1024]{0:T(1024)S(1)}, f32[1024]{0:T(1024)}, u32[]{:S(2)}) %copy-start.3) | copy-done | bytes 4120
  1.3 0.0 copy-start
  1.3 0.9 %copy-done = bf16[1,1024,128]{2,1,0:T(8,128)(2,1)S(1)} copy-done((bf16[1,1024,128]{2,1,0:T(8,128)(2,1)S(1)}, bf16[1,1024,128]{2,1,0:T(8,128)(2,1)}, u32[]{:S(2)}) %copy-start) | copy-done | bytes 262168
  2.3 0.0 copy-start.1
  2.3 0.9 %copy-done.1 = bf16[1,1024,128]{2,1,0:T(8,128)(2,1)S(1)} copy-done((bf16[1,1024,128]{2,1,0:T(8,128)(2,1)S(1)}, bf16[1,1024,128]{2,1,0:T(8,128)(2,1)}, u32[]{:S(2)}) %copy-start.1) | copy-done | bytes 262168
  3.2 0.0 copy-start.2
  3.2 0.8 %copy-done.2 = f32[64,128]{1,0:T(8,128)S(1)} copy-done((f32[64,128]{1,0:T(8,128)S(1)}, f32[64,128]{1,0:T(8,128)}, u32[]{:S(2)}) %copy-start.2) | copy-done | bytes 32792
  4.0 51.7 %shard_map.59 = (bf16[64,16,128]{2,1,0:T(8,128)(2,1)S(1)}, f32[64,128]{1,0:T(8,128)S(1)}) custom-call(bf16[64,16,128]{2,1,0:T(8,128)(2,1)S(1)} %bitcast.4, bf16[64,16,128]{2,1,0:T(8,128)(2,1)S(1)} %bitcast.5, f32[64,128]{1,0:T(8,128)S(1)} %copy-done.2, f32[8,128]{1,0:T(8,128)S(1)} %bitcast.7), custom_call_target="tpu_custom_call" | custom-call | tf_op jit(solution)/shard_map/pallas_call | solution.py:206
  55.7 0.7 %copy.8 = bf16[1,1024,128]{2,1,0:T(8,128)(2,1)} copy(bf16[1,1024,128]{2,1,0:T(8,128)(2,1)S(1)} %bitcast.6) | data formatting | bytes 524288
  56.4 0.6 %copy.9 = f32[64,128]{1,0:T(8,128)} copy(f32[64,128]{1,0:T(8,128)S(1)} %get-tuple-element.9) | data formatting | bytes 65536
Async XLA Ops:
  0.6 0.7 %copy-start.3 = (f32[1024]{0:T(1024)S(1)}, f32[1024]{0:T(1024)}, u32[]{:S(2)}) copy-start(f32[1024]{0:T(1024)} %param.7) | copy-start | bytes 12292
  1.3 0.9 %copy-start = (bf16[1,1024,128]{2,1,0:T(8,128)(2,1)S(1)}, bf16[1,1024,128]{2,1,0:T(8,128)(2,1)}, u32[]{:S(2)}) copy-start(bf16[1,1024,128]{2,1,0:T(8,128)(2,1)} %param.4) | copy-start | bytes 786436
  2.3 0.9 %copy-start.1 = (bf16[1,1024,128]{2,1,0:T(8,128)(2,1)S(1)}, bf16[1,1024,128]{2,1,0:T(8,128)(2,1)}, u32[]{:S(2)}) copy-start(bf16[1,1024,128]{2,1,0:T(8,128)(2,1)} %param.5) | copy-start | bytes 786436
  3.2 0.8 %copy-start.2 = (f32[64,128]{1,0:T(8,128)S(1)}, f32[64,128]{1,0:T(8,128)}, u32[]{:S(2)}) copy-start(f32[64,128]{1,0:T(8,128)} %f_in.1) | copy-start | bytes 98308

commit v2 on v1

v2 whole, which is shorter than its diff:
```python
import functools
import math

import jax
import jax.numpy as jnp
from jax import lax
from jax.experimental import pallas as pl
from jax.experimental.pallas import tpu as pltpu
from jax.sharding import PartitionSpec as P

GROUP = 16
LANES = 128
PAIR = 256
MESH = pl.DeviceIdType.MESH
F32 = jnp.float32
BF16 = jnp.bfloat16

TAPS_LOW, TAPS_HIGH, NEAR_GRAD, NEAR_IN, FAR_GRAD, BACK, TERMS_LOW, TERMS_HIGH, FINAL, TAPS_CROSS = (
    0, 1, 2, 3, 4, 6, 7, 8, 9, 10)
N_SEMS = 11


def whole_wait(ref, sem):
    pltpu.make_async_copy(ref, ref, sem).wait()


def kernel(sizes, x_hbm, g_hbm, f_hbm, s_hbm, gi_out, gf_out,
           f_here, s_here, g_here, f_send, f_all, near, far, x_all, turned, toe, acc, back,
           back_all, direct, lag_rows, lag_send, lag_in, lag_fin, gf_all,
           s_send, s_recv, s_loc, ready):
    owners, seqs, scale = sizes
    half = owners // 2
    own = f_send.shape[1]
    own_groups = own
    blocks = half // 2
    low_taps = half * LANES
    part = owners // seqs
    chunk = own // 2
    me = lax.axis_index("context")
    seq = lax.axis_index("dp")
    z, h = me // half, me % half
    core, place = h % 2, h // 2
    is_low, is_high = z == 0, z == 1

    def send(src, dst, k, where):
        pltpu.make_async_remote_copy(
            src_ref=src, dst_ref=dst, send_sem=s_send.at[k], recv_sem=s_recv.at[k],
            device_id=where, device_id_type=MESH).start()

    def local(src, dst, k):
        pltpu.make_async_copy(src, dst, s_recv.at[k]).start()

    def loop(first, body):
        def step(k, carry):
            body((h + k) % half)
            return carry

        lax.fori_loop(first, half, step, 0)

    def signal(where):
        pl.semaphore_signal(barrier, inc=1, device_id=where, device_id_type=MESH)

    barrier = pltpu.get_barrier_semaphore()
    loop(1, lambda o: signal({"context": z * half + o}))

    @pl.when(is_low)
    def _():
        loop(0, lambda o: signal({"context": half + o}))
        for r in range(1, seqs):
            signal({"dp": (seq + r) % seqs})
            signal({"dp": (seq + r) % seqs, "context": half + h})

    stage = [
        pltpu.make_async_copy(f_hbm, f_here, s_loc.at[0]),
        pltpu.make_async_copy(s_hbm, s_here, s_loc.at[1]),
        pltpu.make_async_copy(g_hbm, g_here, s_loc.at[2]),
    ]
    for copy in stage:
        copy.start()
    mine = pl.ds(own * h, own)
    local(g_hbm.at[mine], near.at[core, :, place], NEAR_GRAD)
    local(x_hbm.at[mine], x_all.at[core, :, place], NEAR_IN)
    zeros = jnp.zeros((2, own, blocks, GROUP, LANES), BF16)

    stage[0].wait()
    for o in range(half):
        f_send[o] = f_here[own * o : own * (o + 1), :]

    @pl.when(is_high)
    def _():
        pl.semaphore_wait(barrier, half - 1 + half + seqs - 1)
        pl.semaphore_signal(ready, inc=1, device_id={"context": h}, device_id_type=MESH)
        loop(0, lambda o: send(f_send.at[o], f_all.at[me], TAPS_HIGH, {"context": o}))
        for c in range(2):
            loop(0, lambda o: send(
                g_hbm.at[pl.ds(own * o + chunk * c, chunk)],
                far.at[core, pl.ds(chunk * c, chunk), blocks + place],
                FAR_GRAD + c, {"context": o}))

    @pl.when(is_low)
    def _():
        pl.semaphore_wait(barrier, half - 1 + seqs - 1)
        loop(1, lambda o: send(f_send.at[o], f_all.at[me], TAPS_LOW, {"context": o}))
        local(f_send.at[h], f_all.at[me], TAPS_LOW)

    loop(1, lambda o: send(
        g_hbm.at[pl.ds(own * o, own)], near.at[core, :, place], NEAR_GRAD,
        {"context": z * half + o}))
    loop(1, lambda o: send(
        x_hbm.at[pl.ds(own * o, own)], x_all.at[core, :, place], NEAR_IN,
        {"context": z * half + o}))

    near[:, :, blocks:] = zeros

    stage[1].wait()
    stage[2].wait()
    by_row = s_here[...].T
    per = LANES // GROUP
    for m in range(s_here.shape[0]):
        piece = g_here[per * m : per * (m + 1)].reshape(LANES, LANES).astype(F32)
        piece = piece * jnp.broadcast_to(by_row[:, m : m + 1], (LANES, LANES))
        direct[per * m : per * (m + 1)] = piece.reshape(per, GROUP, LANES)

    def build(g, first):
        lead = (
            jnp.zeros((GROUP, LANES), F32) if first == 0
            else jnp.broadcast_to(f_all[first - 1, g : g + 1, :], (GROUP, LANES)))
        rows = jnp.concatenate(
            [lead] + [
                jnp.broadcast_to(f_all[j, g : g + 1, :], (GROUP, LANES))
                for j in range(first, first + half)],
            axis=1)
        row = lax.broadcasted_iota(jnp.int32, rows.shape, 0)
        for bit in (1, 2, 4, 8):
            rows = jnp.where(row % (2 * bit) >= bit, pltpu.roll(rows, bit, 1), rows)
        at = LANES * (first + 1)
        if first == 0:
            toe[g, :, 0:LANES] = jnp.zeros((LANES, LANES), BF16)
        for q in range(LANES // GROUP):
            moved = rows if q == 0 else pltpu.roll(rows, GROUP * q, 1)
            toe[g, GROUP * q : GROUP * (q + 1), at : at + low_taps] = (
                moved[:, LANES:].astype(BF16))

    def rows_of(ref, g, start, count):
        return jnp.concatenate(
            [ref[c, g, start : start + count].reshape(count * GROUP, LANES) for c in range(2)],
            axis=1)

    def against_toe(ref, g, first, last, count):
        left = jnp.concatenate([rows_of(ref, g, d, count) for d in range(first, last)], axis=1)
        lo, hi = PAIR * first, PAIR * last
        right = jnp.concatenate(
            [toe[g, :, LANES + lo : LANES + hi], toe[g, :, lo:hi]], axis=0)
        return lax.dot_general(
            left, right, (((1,), (1,)), ((), ())), preferred_element_type=F32)

    def near_correlation(g):
        step = min(4, blocks)
        for e in range(0, blocks, step):
            count = blocks - e
            term = against_toe(near, g, e, e + step, count)
            if e == 0:
                acc[g] = term
            else:
                acc[g, 0 : count * GROUP] += term

    def far_correlation(g):
        total = acc[g]
        for e in range(0, 2 * blocks, 4):
            total = total + against_toe(far, g, e, e + 4, blocks)
        acc[g] = total

    def send_back(first, count):
        for g in range(first, first + count):
            for c in range(2):
                back[c, g] = acc[g, :, LANES * c : LANES * (c + 1)].astype(BF16).reshape(
                    blocks, GROUP, LANES)
        which = pl.ds(first, count)
        where = pl.ds(own * h + first, count)
        local(back.at[core, which, place], back_all.at[where], BACK)
        loop(1, lambda o: send(
            back.at[o % 2, which, o // 2], back_all.at[where], BACK,
            {"context": z * half + o}))

    def near_lags(g):
        left = jnp.concatenate(
            [x_all[c, g].reshape(blocks * GROUP, LANES).T for c in range(2)], axis=0)
        turned[g] = left
        carry = jnp.zeros((LANES, LANES), F32)
        for d in reversed(range(blocks)):
            square = jnp.dot(left, rows_of(near, g, d, blocks), preferred_element_type=F32)
            at = PAIR * d
            lag_rows[g, :, at : at + LANES] = square[:LANES, :LANES] + square[LANES:, LANES:]
            lag_rows[g, :, at + LANES : at + PAIR] = square[:LANES, LANES:] + carry
            carry = square[LANES:, :LANES]

    def far_lags(g):
        left = turned[g]
        carry = jnp.zeros((LANES, LANES), F32)
        for d in reversed(range(1, 2 * blocks)):
            square = jnp.dot(left, rows_of(far, g, d, blocks), preferred_element_type=F32)
            at = PAIR * d
            even = square[:LANES, :LANES] + square[LANES:, LANES:]
            odd = square[:LANES, LANES:] + carry
            if d < blocks:
                even = even + lag_rows[g, :, at : at + LANES]
                odd = odd + lag_rows[g, :, at + LANES : at + PAIR]
            lag_rows[g, :, at : at + LANES] = even
            lag_rows[g, :, at + LANES : at + PAIR] = odd
            carry = square[LANES:, :LANES]
        lag_rows[g, :, LANES:PAIR] += carry

    def diagonals(g, taps):
        width = taps + LANES
        rows = [
            jnp.concatenate(
                [jnp.zeros((8, LANES), F32), lag_rows[g, 8 * q : 8 * (q + 1), :taps]], axis=1)
            for q in range(LANES // 8)]
        move = 8
        while len(rows) > 1:
            rows = [
                rows[k] + pltpu.roll(rows[k + 1], width - move, 1)
                for k in range(0, len(rows), 2)]
            move = 2 * move
        total = rows[0]
        row = lax.broadcasted_iota(jnp.int32, (8, width), 0)
        for bit in (1, 2, 4):
            total = jnp.where(
                row % (2 * bit) >= bit, pltpu.roll(total, width - bit, 1), total)
        line = jnp.sum(total, axis=0, keepdims=True)[:, LANES:]
        for j in range(taps // LANES):
            lag_send[j, g : g + 1, :] = line[:, LANES * j : LANES * (j + 1)]

    @pl.when(is_high)
    def _():
        whole_wait(f_all.at[pl.ds(0, half)], s_recv.at[TAPS_CROSS])
        for g in range(own_groups):
            build(g, 0)
        whole_wait(x_all, s_recv.at[NEAR_GRAD])
        for g in range(own_groups):
            near_correlation(g)
        send_back(0, own)
        whole_wait(x_all, s_recv.at[NEAR_IN])
        for g in range(own_groups):
            near_lags(g)
            diagonals(g, low_taps)
        for p in range(seqs // 2):
            send(lag_send.at[pl.ds(part * p, part)], lag_in.at[1, seq], TERMS_HIGH,
                 {"dp": p, "context": h})
        whole_wait(back_all, s_recv.at[BACK])

    @pl.when(is_low)
    def _():
        far[:, :, 0:blocks] = zeros
        far[:, :, 2 * blocks :] = zeros
        whole_wait(f_all.at[pl.ds(0, half)], s_recv.at[TAPS_LOW])
        for g in range(own_groups):
            build(g, 0)
        pl.semaphore_wait(ready, 1)
        low = f_all.at[pl.ds(0, half)]
        send(low, low, TAPS_CROSS, {"context": half + h})
        whole_wait(x_all, s_recv.at[NEAR_GRAD])
        for g in range(own_groups):
            near_correlation(g)
        whole_wait(x_all, s_recv.at[NEAR_IN])
        for g in range(own_groups):
            near_lags(g)

        whole_wait(f_all.at[pl.ds(half, half)], s_recv.at[TAPS_HIGH])
        for g in range(own_groups):
            build(g, half)
        first = far.at[:, pl.ds(0, chunk), pl.ds(blocks, blocks)]
        whole_wait(first, s_recv.at[FAR_GRAD])
        for g in range(chunk):
            far_correlation(g)
        send_back(0, chunk)
        for g in range(chunk):
            far_lags(g)
            diagonals(g, 2 * low_taps)
        whole_wait(first, s_recv.at[FAR_GRAD + 1])
        for g in range(chunk, own):
            far_lags(g)
            diagonals(g, 2 * low_taps)
        local(lag_send.at[pl.ds(part * seq, part)], lag_in.at[0, seq], TERMS_LOW)
        for r in range(1, seqs):
            p = (seq + r) % seqs
            send(lag_send.at[pl.ds(part * p, part)], lag_in.at[0, seq], TERMS_LOW, {"dp": p})
        for g in range(chunk, own):
            far_correlation(g)
        send_back(chunk, own - chunk)

        whole_wait(lag_in.at[0], s_recv.at[TERMS_LOW])
        summed = lag_in[0, 0]
        for b in range(1, seqs):
            summed = summed + lag_in[0, b]
        lag_fin[...] = summed * scale

        @pl.when(seq < seqs // 2)
        def _():
            whole_wait(lag_in.at[1], s_recv.at[TERMS_HIGH])
            more = lag_in[1, 0]
            for b in range(1, seqs):
                more = more + lag_in[1, b]
            lag_fin[...] += more * scale

        def deliver(k, carry):
            at = seq * part + k % part
            to = (seq + k // part) % seqs

            @pl.when((at != me) | (to != seq))
            def _():
                send(lag_fin.at[k % part], gf_all.at[h], FINAL, {"dp": to, "context": at})

            return carry

        lax.fori_loop(0, owners, deliver, 0)

        @pl.when(me // part == seq)
        def _():
            local(lag_fin.at[me % part], gf_all.at[h], FINAL)

        whole_wait(back_all, s_recv.at[BACK])

    gi_out[...] = (back_all[...].astype(F32) + direct[...]).astype(BF16)
    whole_wait(gf_all, s_recv.at[FINAL])
    for o in range(half):
        gf_out[own * o : own * (o + 1), :] = gf_all[o]

    others = own * (half - 1)
    whole_wait(g_hbm.at[pl.ds(0, others)], s_send.at[NEAR_GRAD])
    whole_wait(x_hbm.at[pl.ds(0, others)], s_send.at[NEAR_IN])
    whole_wait(back_all.at[pl.ds(0, others)], s_send.at[BACK])

    @pl.when(is_high)
    def _():
        whole_wait(f_send, s_send.at[TAPS_HIGH])
        for c in range(2):
            whole_wait(g_hbm.at[pl.ds(0, chunk * half)], s_send.at[FAR_GRAD + c])
        whole_wait(lag_send.at[pl.ds(0, part * (seqs // 2))], s_send.at[TERMS_HIGH])

    @pl.when(is_low)
    def _():
        whole_wait(f_all.at[pl.ds(0, half - 1)], s_send.at[TAPS_LOW])
        whole_wait(f_all.at[pl.ds(0, half)], s_send.at[TAPS_CROSS])
        whole_wait(lag_send.at[pl.ds(0, part * (seqs - 1))], s_send.at[TERMS_LOW])

        @pl.when(me // part == seq)
        def _():
            whole_wait(lag_send.at[pl.ds(0, owners - 1)], s_send.at[FINAL])

        @pl.when(me // part != seq)
        def _():
            whole_wait(lag_send, s_send.at[FINAL])


def per_device(inputs, out_grad, filters, skip):
    channels, tok = inputs.shape[1], inputs.shape[2]
    groups = filters.shape[0]
    owners, seqs = lax.axis_size("context"), lax.axis_size("dp")
    half = owners // 2
    own = groups // half
    blocks = half // 2
    part = owners // seqs
    scale = 1.0 / math.sqrt(seqs * GROUP * tok * owners)
    vmem = pl.BlockSpec(memory_space=pltpu.VMEM)
    hbm = pl.BlockSpec(memory_space=pltpu.HBM)
    tiles = (groups, GROUP, LANES)
    held = (2, own, blocks, GROUP, LANES)
    grad_input, grad_filter = pl.pallas_call(
        functools.partial(kernel, (owners, seqs, scale)),
        out_shape=(
            jax.ShapeDtypeStruct(tiles, BF16),
            jax.ShapeDtypeStruct((groups, LANES), F32),
        ),
        in_specs=[hbm, hbm, hbm, hbm],
        out_specs=(vmem, vmem),
        scratch_shapes=[
            pltpu.VMEM((groups, LANES), F32),
            pltpu.VMEM((channels // LANES, LANES), F32),
            pltpu.VMEM(tiles, BF16),
            pltpu.VMEM((half, own, LANES), F32),
            pltpu.VMEM((owners, own, LANES), F32),
            pltpu.VMEM((2, own, 2 * blocks, GROUP, LANES), BF16),
            pltpu.VMEM((2, own, 3 * blocks, GROUP, LANES), BF16),
            pltpu.VMEM(held, BF16),
            pltpu.VMEM((own, PAIR, blocks * GROUP), BF16),
            pltpu.VMEM((own, LANES, LANES * (owners + 1)), BF16),
            pltpu.VMEM((own, blocks * GROUP, PAIR), F32),
            pltpu.VMEM(held, BF16),
            pltpu.VMEM(tiles, BF16),
            pltpu.VMEM(tiles, F32),
            pltpu.VMEM((own, LANES, LANES * owners), F32),
            pltpu.VMEM((owners, own, LANES), F32),
            pltpu.VMEM((2, seqs, part, own, LANES), F32),
            pltpu.VMEM((part, own, LANES), F32),
            pltpu.VMEM((half, own, LANES), F32),
            pltpu.SemaphoreType.DMA((N_SEMS,)),
            pltpu.SemaphoreType.DMA((N_SEMS,)),
            pltpu.SemaphoreType.DMA((3,)),
            pltpu.SemaphoreType.REGULAR,
        ],
        compiler_params=pltpu.CompilerParams(
            collective_id=0, has_side_effects=True, vmem_limit_bytes=56 * 1024 * 1024),
    )(
        inputs.reshape(tiles),
        out_grad.reshape(tiles),
        filters,
        skip.reshape(channels // LANES, LANES),
    )
    return grad_input.reshape(1, channels, tok), grad_filter


def solution(mesh):
    placed = (
        P("dp", "tensor", "context"),
        P("dp", "tensor", "context"),
        P("tensor", "context"),
        P("tensor"),
    )
    return jax.shard_map(
        per_device,
        mesh=mesh,
        in_specs=placed,
        out_specs=(P("dp", "tensor", "context"), P("tensor", "context")),
        check_vma=False,
    )
```

time: 57.4 us -> 51.1 us (0.89)
  Pallas kernels: 51.7 us -> 48 us
  local copies, waits for them, and re-layouts: 4.66 us -> 2.29 us
    pallas_call x1, Pallas kernels: 51.7 us -> 48 us  [per_device(): pl.pallas_call(functools.partial(kernel, (owners, seqs, scale)), out_shap...]
    unnamed x10 -> x4, local copies, waits for them, and re-layouts: 4.66 us -> 2.29 us
where the time goes in v2:
time: 51.1 us; the launch traced here: 51 us
  Pallas kernels  48 us (94%)
  local copies, waits for them, and re-layouts  2.29 us (4%)
  between operations  0.65 us (1%)
    pallas_call x1, Pallas kernels, per_device(): pl.pallas_call(functools.partial(kernel, (owners, seqs, scale)), out_shap...  48 us
    unnamed x4, local copies, waits for them, and re-layouts  2.29 us

profile of v2, /device:TPU:1, one launch (start us, length us, event | category | flops | bytes accessed | tf_op | source)
XLA Modules:
  0.0 51.0 jit_solution(10180985797823594734)
XLA Ops:
  0.6 48.0 %shard_map.59 = (bf16[64,16,128]{2,1,0:T(8,128)(2,1)}, f32[64,128]{1,0:T(8,128)}) custom-call(bf16[64,16,128]{2,1,0:T(8,128)(2,1)} %bitcast.4, bf16[64,16,128]{2,1,0:T(8,128)(2,1)} %bitcast.5, f32[64,128]{1,0:T(8,128)} %f_hbm.1, f32[8,128]{1,0:T(8,128)} %bitcast.7), custom_call_target="tpu_custom_call" | custom-call | tf_op jit(solution)/shard_map/pallas_call | solution.py:369
  48.6 0.0 copy-start
  48.7 1.7 %copy.8 = bf16[1,1024,128]{2,1,0:T(8,128)(2,1)} copy(bf16[1,1024,128]{2,1,0:T(8,128)(2,1)} %bitcast.6) | data formatting | bytes 524288
  50.3 0.0 copy-done
  50.3 0.6 %copy.9 = f32[64,128]{1,0:T(8,128)} copy(f32[64,128]{1,0:T(8,128)S(1)} %copy-done) | data formatting | bytes 65536
Async XLA Ops:
  48.6 1.7 %copy-start = (f32[64,128]{1,0:T(8,128)S(1)}, f32[64,128]{1,0:T(8,128)}, u32[]{:S(2)}) copy-start(f32[64,128]{1,0:T(8,128)} %get-tuple-element.9) | copy-start | bytes 98308

commit v3 on v2

--- a/solution.py
+++ b/solution.py
@@ -15,9 +15,9 @@
 F32 = jnp.float32
 BF16 = jnp.bfloat16
 
-TAPS_LOW, TAPS_HIGH, NEAR_GRAD, NEAR_IN, FAR_GRAD, BACK, TERMS_LOW, TERMS_HIGH, FINAL, TAPS_CROSS = (
-    0, 1, 2, 3, 4, 6, 7, 8, 9, 10)
-N_SEMS = 11
+TAPS_LOW, TAPS_HIGH, TAPS_CROSS, NEAR_IN, BACK, TERMS_LOW, TERMS_HIGH, FINAL = range(8)
+NEAR_GRAD, FAR_GRAD = 8, 10
+N_SEMS = 12
 
 
 def whole_wait(ref, sem):
@@ -31,11 +31,9 @@
     owners, seqs, scale = sizes
     half = owners // 2
     own = f_send.shape[1]
-    own_groups = own
     blocks = half // 2
     low_taps = half * LANES
     part = owners // seqs
-    chunk = own // 2
     me = lax.axis_index("context")
     seq = lax.axis_index("dp")
     z, h = me // half, me % half
@@ -78,7 +76,10 @@
     for copy in stage:
         copy.start()
     mine = pl.ds(own * h, own)
-    local(g_hbm.at[mine], near.at[core, :, place], NEAR_GRAD)
+    count = own // 2
+    for k in range(2):
+        local(g_hbm.at[pl.ds(own * h + count * k, count)],
+              near.at[core, pl.ds(count * k, count), place], NEAR_GRAD + k)
     local(x_hbm.at[mine], x_all.at[core, :, place], NEAR_IN)
     zeros = jnp.zeros((2, own, blocks, GROUP, LANES), BF16)
 
@@ -91,11 +92,9 @@
         pl.semaphore_wait(barrier, half - 1 + half + seqs - 1)
         pl.semaphore_signal(ready, inc=1, device_id={"context": h}, device_id_type=MESH)
         loop(0, lambda o: send(f_send.at[o], f_all.at[me], TAPS_HIGH, {"context": o}))
-        for c in range(2):
-            loop(0, lambda o: send(
-                g_hbm.at[pl.ds(own * o + chunk * c, chunk)],
-                far.at[core, pl.ds(chunk * c, chunk), blocks + place],
-                FAR_GRAD + c, {"context": o}))
+        loop(0, lambda o: send(
+            g_hbm.at[pl.ds(own * o, count)], far.at[core, pl.ds(0, count), blocks + place],
+            FAR_GRAD, {"context": o}))
 
     @pl.when(is_low)
     def _():
@@ -103,9 +102,11 @@
         loop(1, lambda o: send(f_send.at[o], f_all.at[me], TAPS_LOW, {"context": o}))
         local(f_send.at[h], f_all.at[me], TAPS_LOW)
 
-    loop(1, lambda o: send(
-        g_hbm.at[pl.ds(own * o, own)], near.at[core, :, place], NEAR_GRAD,
-        {"context": z * half + o}))
+    for k in (1, 0):
+        loop(1, lambda o: send(
+            g_hbm.at[pl.ds(own * o + count * k, count)],
+            near.at[core, pl.ds(count * k, count), place], NEAR_GRAD + k,
+            {"context": z * half + o}))
     loop(1, lambda o: send(
         x_hbm.at[pl.ds(own * o, own)], x_all.at[core, :, place], NEAR_IN,
         {"context": z * half + o}))
@@ -231,18 +232,27 @@
         for j in range(taps // LANES):
             lag_send[j, g : g + 1, :] = line[:, LANES * j : LANES * (j + 1)]
 
+    def near_grad(k):
+        return near.at[:, pl.ds(count * k, count), pl.ds(0, blocks)]
+
+    def far_grad(k):
+        return far.at[:, pl.ds(count * k, count), pl.ds(blocks, blocks)]
+
     @pl.when(is_high)
     def _():
+        whole_wait(near_grad(1), s_recv.at[NEAR_GRAD + 1])
+        send(near_grad(1), far_grad(1), FAR_GRAD + 1, {"context": h})
         whole_wait(f_all.at[pl.ds(0, half)], s_recv.at[TAPS_CROSS])
-        for g in range(own_groups):
+        for g in range(own):
             build(g, 0)
-        whole_wait(x_all, s_recv.at[NEAR_GRAD])
-        for g in range(own_groups):
+        whole_wait(near_grad(0), s_recv.at[NEAR_GRAD])
+        for g in range(own):
             near_correlation(g)
         send_back(0, own)
         whole_wait(x_all, s_recv.at[NEAR_IN])
-        for g in range(own_groups):
+        for g in range(own):
             near_lags(g)
+        for g in range(own):
             diagonals(g, low_taps)
         for p in range(seqs // 2):
             send(lag_send.at[pl.ds(part * p, part)], lag_in.at[1, seq], TERMS_HIGH,
@@ -254,40 +264,36 @@
         far[:, :, 0:blocks] = zeros
         far[:, :, 2 * blocks :] = zeros
         whole_wait(f_all.at[pl.ds(0, half)], s_recv.at[TAPS_LOW])
-        for g in range(own_groups):
+        for g in range(own):
             build(g, 0)
         pl.semaphore_wait(ready, 1)
         low = f_all.at[pl.ds(0, half)]
         send(low, low, TAPS_CROSS, {"context": half + h})
-        whole_wait(x_all, s_recv.at[NEAR_GRAD])
-        for g in range(own_groups):
-            near_correlation(g)
+        for k in (1, 0):
+            whole_wait(near_grad(k), s_recv.at[NEAR_GRAD + k])
+            for g in range(count * k, count * (k + 1)):
+                near_correlation(g)
+        whole_wait(f_all.at[pl.ds(half, half)], s_recv.at[TAPS_HIGH])
+        for g in range(own):
+            build(g, half)
         whole_wait(x_all, s_recv.at[NEAR_IN])
-        for g in range(own_groups):
+        for g in range(own):
             near_lags(g)
-
-        whole_wait(f_all.at[pl.ds(half, half)], s_recv.at[TAPS_HIGH])
-        for g in range(own_groups):
-            build(g, half)
-        first = far.at[:, pl.ds(0, chunk), pl.ds(blocks, blocks)]
-        whole_wait(first, s_recv.at[FAR_GRAD])
-        for g in range(chunk):
-            far_correlation(g)
-        send_back(0, chunk)
-        for g in range(chunk):
-            far_lags(g)
-            diagonals(g, 2 * low_taps)
-        whole_wait(first, s_recv.at[FAR_GRAD + 1])
-        for g in range(chunk, own):
-            far_lags(g)
-            diagonals(g, 2 * low_taps)
+        pairs = (range(0, count), range(count, own))
+        for k, some in enumerate(pairs):
+            whole_wait(far_grad(k), s_recv.at[FAR_GRAD + k])
+            for g in some:
+                far_lags(g)
+            for g in some:
+                diagonals(g, 2 * low_taps)
         local(lag_send.at[pl.ds(part * seq, part)], lag_in.at[0, seq], TERMS_LOW)
         for r in range(1, seqs):
             p = (seq + r) % seqs
             send(lag_send.at[pl.ds(part * p, part)], lag_in.at[0, seq], TERMS_LOW, {"dp": p})
-        for g in range(chunk, own):
-            far_correlation(g)
-        send_back(chunk, own - chunk)
+        for some in pairs:
+            for g in some:
+                far_correlation(g)
+            send_back(some[0], len(some))
 
         whole_wait(lag_in.at[0], s_recv.at[TERMS_LOW])
         summed = lag_in[0, 0]
@@ -327,15 +333,16 @@
         gf_out[own * o : own * (o + 1), :] = gf_all[o]
 
     others = own * (half - 1)
-    whole_wait(g_hbm.at[pl.ds(0, others)], s_send.at[NEAR_GRAD])
+    for k in range(2):
+        whole_wait(g_hbm.at[pl.ds(0, count * (half - 1))], s_send.at[NEAR_GRAD + k])
     whole_wait(x_hbm.at[pl.ds(0, others)], s_send.at[NEAR_IN])
     whole_wait(back_all.at[pl.ds(0, others)], s_send.at[BACK])
 
     @pl.when(is_high)
     def _():
         whole_wait(f_send, s_send.at[TAPS_HIGH])
-        for c in range(2):
-            whole_wait(g_hbm.at[pl.ds(0, chunk * half)], s_send.at[FAR_GRAD + c])
+        for k in range(2):
+            whole_wait(near_grad(k), s_send.at[FAR_GRAD + k])
         whole_wait(lag_send.at[pl.ds(0, part * (seqs // 2))], s_send.at[TERMS_HIGH])
 
     @pl.when(is_low)
@@ -351,6 +358,10 @@
         @pl.when(me // part != seq)
         def _():
             whole_wait(lag_send, s_send.at[FINAL])
+
+
+def stay(array):
+    return pltpu.with_memory_space_constraint(array, pltpu.HBM)
 
 
 def per_device(inputs, out_grad, filters, skip):
@@ -400,12 +411,12 @@
             pltpu.SemaphoreType.REGULAR,
         ],
         compiler_params=pltpu.CompilerParams(
-            collective_id=0, has_side_effects=True, vmem_limit_bytes=56 * 1024 * 1024),
+            collective_id=0, has_side_effects=True, vmem_limit_bytes=28 * 1024 * 1024),
     )(
-        inputs.reshape(tiles),
-        out_grad.reshape(tiles),
-        filters,
-        skip.reshape(channels // LANES, LANES),
+        stay(inputs.reshape(tiles)),
+        stay(out_grad.reshape(tiles)),
+        stay(filters),
+        stay(skip.reshape(channels // LANES, LANES)),
     )
     return grad_input.reshape(1, channels, tok), grad_filter
 

time: 51.1 us -> 47.6 us (0.932)
  the two profiles are of different devices: /device:TPU:1 before, /device:TPU:53 now
where the time goes in v3:
time: 47.6 us; the launch traced here: 47.5 us
  Pallas kernels  45.5 us (96%)
  local copies, waits for them, and re-layouts  1.32 us (3%)
  between operations  0.64 us (1%)
    pallas_call x1, Pallas kernels, per_device(): pl.pallas_call(functools.partial(kernel, (owners, seqs, scale)), out_shap...  45.5 us
    unnamed x2, local copies, waits for them, and re-layouts  1.32 us

profile of v3, /device:TPU:53, one launch (start us, length us, event | category | flops | bytes accessed | tf_op | source)
XLA Modules:
  0.0 47.5 jit_solution(12889914083886740605)
XLA Ops:
  0.6 45.5 %shard_map.59 = (bf16[64,16,128]{2,1,0:T(8,128)(2,1)S(1)}, f32[64,128]{1,0:T(8,128)S(1)}) custom-call(bf16[64,16,128]{2,1,0:T(8,128)(2,1)} %bitcast.5, bf16[64,16,128]{2,1,0:T(8,128)(2,1)} %bitcast.6, f32[64,128]{1,0:T(8,128)} %f_hbm.1, f32[8,128]{1,0:T(8,128)} %bitcast.7), custom_call_target="tpu_custom_call" | custom-call | tf_op jit(solution)/shard_map/pallas_call | solution.py:380
  46.2 0.7 %copy.8 = bf16[1,1024,128]{2,1,0:T(8,128)(2,1)} copy(bf16[1,1024,128]{2,1,0:T(8,128)(2,1)S(1)} %bitcast.4) | data formatting | bytes 524288
  46.9 0.6 %copy.9 = f32[64,128]{1,0:T(8,128)} copy(f32[64,128]{1,0:T(8,128)S(1)} %get-tuple-element.9) | data formatting | bytes 65536

commit v4 on v3

--- a/solution.py
+++ b/solution.py
@@ -15,9 +15,9 @@
 F32 = jnp.float32
 BF16 = jnp.bfloat16
 
-TAPS_LOW, TAPS_HIGH, TAPS_CROSS, NEAR_IN, BACK, TERMS_LOW, TERMS_HIGH, FINAL = range(8)
-NEAR_GRAD, FAR_GRAD = 8, 10
-N_SEMS = 12
+TAPS_LOW, TAPS_HIGH, TAPS_CROSS, BACK, TERMS_LOW, TERMS_HIGH, FINAL = range(7)
+NEAR_GRAD, NEAR_IN, FAR_GRAD = 7, 9, 11
+N_SEMS = 13
 
 
 def whole_wait(ref, sem):
@@ -75,12 +75,25 @@
     ]
     for copy in stage:
         copy.start()
-    mine = pl.ds(own * h, own)
     count = own // 2
     for k in range(2):
         local(g_hbm.at[pl.ds(own * h + count * k, count)],
               near.at[core, pl.ds(count * k, count), place], NEAR_GRAD + k)
-    local(x_hbm.at[mine], x_all.at[core, :, place], NEAR_IN)
+        local(x_hbm.at[pl.ds(own * h + count * k, count)],
+              x_all.at[core, pl.ds(count * k, count), place], NEAR_IN + k)
+
+    def send_grad(k):
+        loop(1, lambda o: send(
+            g_hbm.at[pl.ds(own * o + count * k, count)],
+            near.at[core, pl.ds(count * k, count), place], NEAR_GRAD + k,
+            {"context": z * half + o}))
+
+    def send_in(k):
+        loop(1, lambda o: send(
+            x_hbm.at[pl.ds(own * o + count * k, count)],
+            x_all.at[core, pl.ds(count * k, count), place], NEAR_IN + k,
+            {"context": z * half + o}))
+
     zeros = jnp.zeros((2, own, blocks, GROUP, LANES), BF16)
 
     stage[0].wait()
@@ -95,21 +108,20 @@
         loop(0, lambda o: send(
             g_hbm.at[pl.ds(own * o, count)], far.at[core, pl.ds(0, count), blocks + place],
             FAR_GRAD, {"context": o}))
+        send_grad(1)
+        send_in(1)
+        send_grad(0)
+        send_in(0)
 
     @pl.when(is_low)
     def _():
         pl.semaphore_wait(barrier, half - 1 + seqs - 1)
         loop(1, lambda o: send(f_send.at[o], f_all.at[me], TAPS_LOW, {"context": o}))
         local(f_send.at[h], f_all.at[me], TAPS_LOW)
-
-    for k in (1, 0):
-        loop(1, lambda o: send(
-            g_hbm.at[pl.ds(own * o + count * k, count)],
-            near.at[core, pl.ds(count * k, count), place], NEAR_GRAD + k,
-            {"context": z * half + o}))
-    loop(1, lambda o: send(
-        x_hbm.at[pl.ds(own * o, own)], x_all.at[core, :, place], NEAR_IN,
-        {"context": z * half + o}))
+        send_grad(0)
+        send_grad(1)
+        send_in(0)
+        send_in(1)
 
     near[:, :, blocks:] = zeros
 
@@ -235,6 +247,9 @@
     def near_grad(k):
         return near.at[:, pl.ds(count * k, count), pl.ds(0, blocks)]
 
+    def near_in(k):
+        return x_all.at[:, pl.ds(count * k, count)]
+
     def far_grad(k):
         return far.at[:, pl.ds(count * k, count), pl.ds(blocks, blocks)]
 
@@ -245,14 +260,19 @@
         whole_wait(f_all.at[pl.ds(0, half)], s_recv.at[TAPS_CROSS])
         for g in range(own):
             build(g, 0)
+        whole_wait(near_in(1), s_recv.at[NEAR_IN + 1])
+        for g in range(count, own):
+            near_lags(g)
+        for g in range(count, own):
+            diagonals(g, low_taps)
         whole_wait(near_grad(0), s_recv.at[NEAR_GRAD])
         for g in range(own):
             near_correlation(g)
         send_back(0, own)
-        whole_wait(x_all, s_recv.at[NEAR_IN])
-        for g in range(own):
+        whole_wait(near_in(0), s_recv.at[NEAR_IN])
+        for g in range(count):
             near_lags(g)
-        for g in range(own):
+        for g in range(count):
             diagonals(g, low_taps)
         for p in range(seqs // 2):
             send(lag_send.at[pl.ds(part * p, part)], lag_in.at[1, seq], TERMS_HIGH,
@@ -269,31 +289,40 @@
         pl.semaphore_wait(ready, 1)
         low = f_all.at[pl.ds(0, half)]
         send(low, low, TAPS_CROSS, {"context": half + h})
-        for k in (1, 0):
+        for k in range(2):
             whole_wait(near_grad(k), s_recv.at[NEAR_GRAD + k])
             for g in range(count * k, count * (k + 1)):
                 near_correlation(g)
         whole_wait(f_all.at[pl.ds(half, half)], s_recv.at[TAPS_HIGH])
         for g in range(own):
             build(g, half)
-        whole_wait(x_all, s_recv.at[NEAR_IN])
-        for g in range(own):
+        early, late = range(0, count), range(count, own)
+        whole_wait(near_in(0), s_recv.at[NEAR_IN])
+        for g in early:
             near_lags(g)
-        pairs = (range(0, count), range(count, own))
-        for k, some in enumerate(pairs):
-            whole_wait(far_grad(k), s_recv.at[FAR_GRAD + k])
-            for g in some:
-                far_lags(g)
-            for g in some:
-                diagonals(g, 2 * low_taps)
+        whole_wait(far_grad(0), s_recv.at[FAR_GRAD])
+        for g in early:
+            far_lags(g)
+        for g in early:
+            diagonals(g, 2 * low_taps)
+        whole_wait(near_in(1), s_recv.at[NEAR_IN + 1])
+        for g in late:
+            near_lags(g)
+        for g in early:
+            far_correlation(g)
+        send_back(0, count)
+        whole_wait(far_grad(1), s_recv.at[FAR_GRAD + 1])
+        for g in late:
+            far_lags(g)
+        for g in late:
+            diagonals(g, 2 * low_taps)
         local(lag_send.at[pl.ds(part * seq, part)], lag_in.at[0, seq], TERMS_LOW)
         for r in range(1, seqs):
             p = (seq + r) % seqs
             send(lag_send.at[pl.ds(part * p, part)], lag_in.at[0, seq], TERMS_LOW, {"dp": p})
-        for some in pairs:
-            for g in some:
-                far_correlation(g)
-            send_back(some[0], len(some))
+        for g in late:
+            far_correlation(g)
+        send_back(count, own - count)
 
         whole_wait(lag_in.at[0], s_recv.at[TERMS_LOW])
         summed = lag_in[0, 0]
@@ -335,7 +364,7 @@
     others = own * (half - 1)
     for k in range(2):
         whole_wait(g_hbm.at[pl.ds(0, count * (half - 1))], s_send.at[NEAR_GRAD + k])
-    whole_wait(x_hbm.at[pl.ds(0, others)], s_send.at[NEAR_IN])
+        whole_wait(x_hbm.at[pl.ds(0, count * (half - 1))], s_send.at[NEAR_IN + k])
     whole_wait(back_all.at[pl.ds(0, others)], s_send.at[BACK])
 
     @pl.when(is_high)

time: 47.6 us -> 46.5 us (0.977)
  the two profiles are of different devices: /device:TPU:53 before, /device:TPU:1 now
where the time goes in v4:
time: 46.5 us; the launch traced here: 46.4 us
  Pallas kernels  44.4 us (95%)
  local copies, waits for them, and re-layouts  1.32 us (3%)
  between operations  0.64 us (1%)
    pallas_call x1, Pallas kernels, per_device(): pl.pallas_call(functools.partial(kernel, (owners, seqs, scale)), out_shap...  44.4 us
    unnamed x2, local copies, waits for them, and re-layouts  1.32 us

profile of v4, /device:TPU:1, one launch (start us, length us, event | category | flops | bytes accessed | tf_op | source)
XLA Modules:
  0.0 46.4 jit_solution(8688322188448345226)
XLA Ops:
  0.6 44.4 %shard_map.59 = (bf16[64,16,128]{2,1,0:T(8,128)(2,1)S(1)}, f32[64,128]{1,0:T(8,128)S(1)}) custom-call(bf16[64,16,128]{2,1,0:T(8,128)(2,1)} %bitcast.5, bf16[64,16,128]{2,1,0:T(8,128)(2,1)} %bitcast.6, f32[64,128]{1,0:T(8,128)} %f_hbm.1, f32[8,128]{1,0:T(8,128)} %bitcast.7), custom_call_target="tpu_custom_call" | custom-call | tf_op jit(solution)/shard_map/pallas_call | solution.py:409
  45.1 0.7 %copy.8 = bf16[1,1024,128]{2,1,0:T(8,128)(2,1)} copy(bf16[1,1024,128]{2,1,0:T(8,128)(2,1)S(1)} %bitcast.4) | data formatting | bytes 524288
  45.8 0.6 %copy.9 = f32[64,128]{1,0:T(8,128)} copy(f32[64,128]{1,0:T(8,128)S(1)} %get-tuple-element.9) | data formatting | bytes 65536

commit v5 on v4

--- a/solution.py
+++ b/solution.py
@@ -17,7 +17,7 @@
 
 TAPS_LOW, TAPS_HIGH, TAPS_CROSS, BACK, TERMS_LOW, TERMS_HIGH, FINAL = range(7)
 NEAR_GRAD, NEAR_IN, FAR_GRAD = 7, 9, 11
-N_SEMS = 13
+N_SEMS = 14
 
 
 def whole_wait(ref, sem):
@@ -58,16 +58,6 @@
     def signal(where):
         pl.semaphore_signal(barrier, inc=1, device_id=where, device_id_type=MESH)
 
-    barrier = pltpu.get_barrier_semaphore()
-    loop(1, lambda o: signal({"context": z * half + o}))
-
-    @pl.when(is_low)
-    def _():
-        loop(0, lambda o: signal({"context": half + o}))
-        for r in range(1, seqs):
-            signal({"dp": (seq + r) % seqs})
-            signal({"dp": (seq + r) % seqs, "context": half + h})
-
     stage = [
         pltpu.make_async_copy(f_hbm, f_here, s_loc.at[0]),
         pltpu.make_async_copy(s_hbm, s_here, s_loc.at[1]),
@@ -75,6 +65,17 @@
     ]
     for copy in stage:
         copy.start()
+
+    barrier = pltpu.get_barrier_semaphore()
+    loop(1, lambda o: signal({"context": z * half + o}))
+
+    @pl.when(is_low)
+    def _():
+        loop(0, lambda o: signal({"context": half + o}))
+        for r in range(1, seqs):
+            signal({"dp": (seq + r) % seqs})
+            signal({"dp": (seq + r) % seqs, "context": half + h})
+
     count = own // 2
     for k in range(2):
         local(g_hbm.at[pl.ds(own * h + count * k, count)],
@@ -250,13 +251,15 @@
     def near_in(k):
         return x_all.at[:, pl.ds(count * k, count)]
 
-    def far_grad(k):
-        return far.at[:, pl.ds(count * k, count), pl.ds(blocks, blocks)]
+    def far_grad(g, n):
+        return far.at[:, pl.ds(g, n), pl.ds(blocks, blocks)]
 
     @pl.when(is_high)
     def _():
         whole_wait(near_grad(1), s_recv.at[NEAR_GRAD + 1])
-        send(near_grad(1), far_grad(1), FAR_GRAD + 1, {"context": h})
+        for g in range(count, own):
+            send(near.at[:, pl.ds(g, 1), pl.ds(0, blocks)], far_grad(g, 1),
+                 FAR_GRAD + 1 + g - count, {"context": h})
         whole_wait(f_all.at[pl.ds(0, half)], s_recv.at[TAPS_CROSS])
         for g in range(own):
             build(g, 0)
@@ -300,7 +303,7 @@
         whole_wait(near_in(0), s_recv.at[NEAR_IN])
         for g in early:
             near_lags(g)
-        whole_wait(far_grad(0), s_recv.at[FAR_GRAD])
+        whole_wait(far_grad(0, count), s_recv.at[FAR_GRAD])
         for g in early:
             far_lags(g)
         for g in early:
@@ -311,10 +314,9 @@
         for g in early:
             far_correlation(g)
         send_back(0, count)
-        whole_wait(far_grad(1), s_recv.at[FAR_GRAD + 1])
         for g in late:
+            whole_wait(far_grad(g, 1), s_recv.at[FAR_GRAD + 1 + g - count])
             far_lags(g)
-        for g in late:
             diagonals(g, 2 * low_taps)
         local(lag_send.at[pl.ds(part * seq, part)], lag_in.at[0, seq], TERMS_LOW)
         for r in range(1, seqs):
@@ -370,8 +372,9 @@
     @pl.when(is_high)
     def _():
         whole_wait(f_send, s_send.at[TAPS_HIGH])
-        for k in range(2):
-            whole_wait(near_grad(k), s_send.at[FAR_GRAD + k])
+        whole_wait(near_grad(0), s_send.at[FAR_GRAD])
+        for g in range(count, own):
+            whole_wait(far_grad(g, 1), s_send.at[FAR_GRAD + 1 + g - count])
         whole_wait(lag_send.at[pl.ds(0, part * (seqs // 2))], s_send.at[TERMS_HIGH])
 
     @pl.when(is_low)

time: 46.5 us -> 46.2 us (level)
  no operation moved by 1% of the time
where the time goes in v5:
time: 46.2 us; the launch traced here: 46.1 us
  Pallas kernels  44.1 us (95%)
  local copies, waits for them, and re-layouts  1.32 us (3%)
  between operations  0.64 us (1%)
    pallas_call x1, Pallas kernels, per_device(): pl.pallas_call(functools.partial(kernel, (owners, seqs, scale)), out_shap...  44.1 us
    unnamed x2, local copies, waits for them, and re-layouts  1.32 us

profile of v5, /device:TPU:1, one launch (start us, length us, event | category | flops | bytes accessed | tf_op | source)
XLA Modules:
  0.0 46.1 jit_solution(16005392812901023231)
XLA Ops:
  0.6 44.1 %shard_map.59 = (bf16[64,16,128]{2,1,0:T(8,128)(2,1)S(1)}, f32[64,128]{1,0:T(8,128)S(1)}) custom-call(bf16[64,16,128]{2,1,0:T(8,128)(2,1)} %bitcast.5, bf16[64,16,128]{2,1,0:T(8,128)(2,1)} %bitcast.6, f32[64,128]{1,0:T(8,128)} %f_hbm.1, f32[8,128]{1,0:T(8,128)} %bitcast.7), custom_call_target="tpu_custom_call" | custom-call | tf_op jit(solution)/shard_map/pallas_call | solution.py:412
  44.8 0.7 %copy.8 = bf16[1,1024,128]{2,1,0:T(8,128)(2,1)} copy(bf16[1,1024,128]{2,1,0:T(8,128)(2,1)S(1)} %bitcast.4) | data formatting | bytes 524288
  45.5 0.6 %copy.9 = f32[64,128]{1,0:T(8,128)} copy(f32[64,128]{1,0:T(8,128)S(1)} %get-tuple-element.9) | data formatting | bytes 65536

commit v6 on v5

--- a/solution.py
+++ b/solution.py
@@ -50,10 +50,11 @@
 
     def loop(first, body):
         def step(k, carry):
-            body((h + k) % half)
+            away = half // 2 + (k + 1) // 2 * (2 * (k % 2) - 1)
+            body((h + away) % half)
             return carry
 
-        lax.fori_loop(first, half, step, 0)
+        lax.fori_loop(0, half - first, step, 0)
 
     def signal(where):
         pl.semaphore_signal(barrier, inc=1, device_id=where, device_id_type=MESH)

time: 46.2 us -> 45.2 us (0.978)
  Pallas kernels: 44.1 us -> 43.2 us
    pallas_call x1, Pallas kernels: 44.1 us -> 43.2 us  [per_device(): pl.pallas_call(functools.partial(kernel, (owners, seqs, scale)), out_shap...]
where the time goes in v6:
time: 45.2 us; the launch traced here: 45.1 us
  Pallas kernels  43.2 us (96%)
  local copies, waits for them, and re-layouts  1.32 us (3%)
  between operations  0.64 us (1%)
    pallas_call x1, Pallas kernels, per_device(): pl.pallas_call(functools.partial(kernel, (owners, seqs, scale)), out_shap...  43.2 us
    unnamed x2, local copies, waits for them, and re-layouts  1.32 us

profile of v6, /device:TPU:1, one launch (start us, length us, event | category | flops | bytes accessed | tf_op | source)
XLA Modules:
  0.0 45.1 jit_solution(8269491234620408614)
XLA Ops:
  0.6 43.2 %shard_map.59 = (bf16[64,16,128]{2,1,0:T(8,128)(2,1)S(1)}, f32[64,128]{1,0:T(8,128)S(1)}) custom-call(bf16[64,16,128]{2,1,0:T(8,128)(2,1)} %bitcast.5, bf16[64,16,128]{2,1,0:T(8,128)(2,1)} %bitcast.6, f32[64,128]{1,0:T(8,128)} %f_hbm.1, f32[8,128]{1,0:T(8,128)} %bitcast.7), custom_call_target="tpu_custom_call" | custom-call | tf_op jit(solution)/shard_map/pallas_call | solution.py:413
  43.8 0.7 %copy.8 = bf16[1,1024,128]{2,1,0:T(8,128)(2,1)} copy(bf16[1,1024,128]{2,1,0:T(8,128)(2,1)S(1)} %bitcast.4) | data formatting | bytes 524288
  44.5 0.6 %copy.9 = f32[64,128]{1,0:T(8,128)} copy(f32[64,128]{1,0:T(8,128)S(1)} %get-tuple-element.9) | data formatting | bytes 65536
